TPU v7x, 1024 devices: a whole 8x8x8 slice. The times are simulated.
1024 devices in a mesh: chan: 32 (over x, y_lo, core), blk: 32 (over z, y_hi).
Axes of the slice: x: 8, y: 8 (y_hi: 4, y_lo: 2; y = y_hi * 2 + y_lo), z: 8, core: 2. Of those that a mesh axis runs over, the one named last changes fastest.
Arguments:
- t_matrix: bfloat16 [32, 4096, 1024], P('chan', 'blk'), may hold values from -0.1875 to 0.1875
- v_jacobi: bfloat16 [32, 1024, 1024], P('chan'), may hold values from -6 to 6
- channel_dims: int32 [32], P('chan'), may hold values from 128 to 1024, as said below
- owner_map: int32 [32], replicated, may hold values from 0 to 31, each once
Outputs:
- triplet_blocks: bfloat16 [32, 32, 4096, 128], P('chan', None, 'blk')
Inputs may be any that keep to these rules, and one draw needn't show every extreme that they name: `channel_dims`: channel 0 has exactly 1024 live states; others vary.
All inputs are finite; a program needn't handle non-finite values.
Results may differ from a plain program's by a relative error of at most 0.0058.
Values may be sent and summed in bfloat16 or wider, within the bound.
A program may use at most 64 MiB of HBM per device.

v0:
```python
import jax
import jax.numpy as jnp
from jax import lax
from jax.sharding import PartitionSpec as P


def per_device(t_matrix, v_jacobi, channel_dims, owner_map):
    jac_width = v_jacobi.shape[2]
    positions = jnp.arange(jac_width, dtype=jnp.int32)
    kept_mask = (positions[None, :] < channel_dims[:, None]).astype(jnp.float32)
    v_float = v_jacobi.astype(jnp.float32)
    v_masked = (
        (v_float + jnp.swapaxes(v_float, 1, 2))
        * 0.5
        * kept_mask[:, :, None]
        * kept_mask[:, None, :]
    ).astype(jnp.bfloat16)
    weighted = jnp.einsum(
        "crj,cji->cri", t_matrix, v_masked, preferred_element_type=jnp.float32
    ).astype(jnp.bfloat16)
    groups = lax.axis_size("chan")
    owners = jnp.arange(groups, dtype=jnp.int32)
    source_block = jnp.sum(
        owners[None, :] * (owner_map[None, :] == owners[:, None]).astype(jnp.int32), axis=1
    )
    lab_rows = jnp.einsum(
        "cri,cpi->crp",
        weighted,
        lax.all_gather(t_matrix, "blk", axis=1, tiled=True),
        preferred_element_type=jnp.float32,
    ).astype(jnp.bfloat16)
    block_cols = lab_rows.shape[2] // groups
    col_blocks = lab_rows.reshape(lab_rows.shape[0], lab_rows.shape[1], groups, block_cols)
    picked = jnp.take(col_blocks, source_block, axis=2)
    outgoing = jnp.transpose(picked, (2, 0, 1, 3))
    return lax.all_to_all(outgoing, "chan", split_axis=0, concat_axis=1, tiled=True)


def solution(mesh):
    in_specs = (P("chan", "blk", None), P("chan", None, None), P("chan"), P())
    out_specs = P("chan", None, "blk", None)
    return jax.shard_map(
        per_device, mesh=mesh, in_specs=in_specs, out_specs=out_specs, check_vma=False
    )
```

profile of v0, /device:TPU:1, one launch (start us, length us, event | category | flops | bytes accessed | tf_op | source)
XLA Modules:
  0.0 224.8 jit_solution(7091776327395734611)
XLA Ops:
  6.5 0.0 copy-start.1
  6.5 0.0 copy-start
  6.5 0.0 copy-start.2
  6.5 0.0 all-gather.2.cloned.1.call-start
  6.5 0.7 all-gather.2.cloned.1.call-update
  7.9 4.1 %copy.11 = f32[1,1024,1024]{1,2,0:T(8,128)} copy(bf16[1,1024,1024]{2,1,0:T(8,128)(2,1)} %param.5) | data formatting | bytes 6291456 | tf_op jit(solution)/shard_map/convert_element_type | solution.py:11
  12.1 0.0 copy-done.2
  12.1 0.1 select_reduce_fusion
  12.2 154.7 %all-gather.2.cloned.1.call-done = bf16[1,4096,1024]{2,1,0:T(8,128)(2,1)} async-done(((bf16[1,128,1024]{2,1,0:T(8,128)(2,1)}), bf16[1,4096,1024]{2,1,0:T(8,128)(2,1)}) %all-gather.2.cloned.1.call-update) | async-done | bytes 8388624 | tf_op jit(solution)/shard_map/all_gather | solution.py:29
  166.9 0.0 copy-done.1
  166.9 0.0 copy-done
  166.9 9.2 %fusion.13 = bf16[16,32,8,128]{3,2,1,0:T(8,128)(2,1)S(1)} fusion(bf16[1,4096,1024]{2,1,0:T(8,128)(2,1)} %all-gather.2.cloned.1.call-done, f32[1,1024,1024]{1,2,0:T(8,128)} %copy.11, f32[1024]{0:T(1024)S(1)} %fusion.25, f32[1024]{0:T(1024)S(1)} %fusion.26, bf16[1,1024,1024]{2,1,0:T(8,128)(2,1)S(1)} %copy-done, bf16[1,128,1024]{2,1,0:T(8,128)(2,1)S(1)} %copy-done.1), kind=kOutput, calls=%fused_computation.12 | convolution fusion | flops 1348075520 | bytes 15998976 | tf_op jit(solution)/shard_map/cri,cpi->crp/dot_general | solution.py:26
  176.1 0.3 copy.16
  176.4 0.8 gather_fusion
  177.2 0.2 fusion.19
  177.4 39.6 %all_to_all.12 = bf16[32,1,128,128]{3,2,1,0:T(8,128)(2,1)S(1)} all-to-all(bf16[32,1,128,128]{3,2,1,0:T(8,128)(2,1)S(1)} %fusion.19), channel_id=1, replica_groups=mesh['chan'=32,'blk'=32] {'chan'}, dimensions={0} | all-to-all | bytes 2097152 | tf_op jit(solution)/shard_map/all_to_all | solution.py:36
  217.0 1.0 copy.19
  (5 shorter events, 0.0 us)
Async XLA Ops:
  6.5 160.4 %copy-start.1 = (bf16[1,128,1024]{2,1,0:T(8,128)(2,1)S(1)}, bf16[1,128,1024]{2,1,0:T(8,128)(2,1)}, u32[]{:S(2)}) copy-start(bf16[1,128,1024]{2,1,0:T(8,128)(2,1)} %param.4) | copy-start | bytes 786436
  6.5 160.4 %copy-start = (bf16[1,1024,1024]{2,1,0:T(8,128)(2,1)S(1)}, bf16[1,1024,1024]{2,1,0:T(8,128)(2,1)}, u32[]{:S(2)}) copy-start(bf16[1,1024,1024]{2,1,0:T(8,128)(2,1)} %param.5) | copy-start | bytes 6291460
  6.5 5.5 %copy-start.2 = (s32[32]{0:T(128)S(1)}, s32[32]{0:T(128)}, u32[]{:S(2)}) copy-start(s32[32]{0:T(128)} %param.7) | copy-start | bytes 388
  6.5 160.4 %all-gather.2.cloned.1.call-start = ((), (), s32[]{:S(2)}) async-start(), calls=%async_computation.1 | async-start | bytes 8650752 | tf_op jit(solution)/shard_map/all_gather | solution.py:29
Sparse Core Ops, SparseCore 0:
  11.7 155.1 all-gather.1
where the time goes:
time: 225 us
  waiting for transfers between devices  155 us (69%)
  blocking collectives  39.6 us (18%)
  between operations  14.1 us (6%)
  matrix products  9.23 us (4%)
  local copies, waits for them, and re-layouts  6.14 us (3%)
    all_gather x1, waiting for transfers between devices, per_device(): lax.all_gather(t_matrix, 'blk', axis=1, tiled=True)  155 us
    all_to_all x1, blocking collectives, per_device(): lax.all_to_all(outgoing, 'chan', split_axis=0, concat_axis=1, tiled=True)  39.6 us
    dot_general x1, matrix products, per_device(): jnp.einsum('cri,cpi->crp', weighted, lax.all_gather(t_matrix, 'blk', axis...  9.23 us
  transfers between devices with their start and end apart: 1, of which 1 were waited for; matrix products, arithmetic and copies ran while one was open for 2% of the time, Pallas kernels for 0%

commit v1 on v0

v1 whole, which is shorter than its diff:
```python
import jax
import jax.numpy as jnp
from jax import lax
from jax.experimental import pallas as pl
from jax.experimental.pallas import tpu as pltpu
from jax.sharding import PartitionSpec as P

MESH = pl.DeviceIdType.MESH
NZ, NY = 8, 4
NX, NL, NC = 8, 2, 2
NCHAN = NX * NL * NC
ROWS, JAC, CB = 128, 1024, 128
PIECES = 4
PROWS = ROWS // PIECES
CHUNKS = 4
CROWS = ROWS // CHUNKS
Z_SHIFTS = (6, 7, 1, 2)
Y_SHIFTS = (1, 2, 3)
FAR = (3, 4, 5)
OWN = len(Z_SHIFTS)


def kernel(
    t_ref,
    v_ref,
    dims_ref,
    owner_ref,
    out_ref,
    tz,
    ty,
    v_raw,
    v_sym,
    wts,
    z_out,
    y_out,
    *rest,
):
    got = rest[:CHUNKS]
    stage = rest[CHUNKS : 2 * CHUNKS]
    (
        slots,
        local_sem,
        zs_sem,
        zr_sem,
        ys_sem,
        yr_sem,
        xs_sem,
        xr_sem,
        os_sem,
        or_sem,
    ) = rest[2 * CHUNKS :]

    chan = lax.axis_index("chan")
    blk = lax.axis_index("blk")
    z, y = blk // NY, blk % NY
    x, lo, core = chan // (NL * NC), (chan // NC) % NL, chan % NC

    def z_peer(shift):
        return (chan, ((z + shift) % NZ) * NY + y)

    def y_peer(shift):
        return (chan, z * NY + (y + shift) % NY)

    def owner_at(i):
        k, b = i % NX, 3 - i // NX
        dx = NX // 2 + (1 - 2 * (k % 2)) * ((k + 1) // 2)
        return (((x + dx) % NX) * NL + (lo + b // 2) % NL) * NC + (core + b % 2) % NC

    load_t = pltpu.make_async_copy(t_ref.at[0], tz.at[0], local_sem.at[0])
    load_v = pltpu.make_async_copy(v_ref.at[0], v_raw, local_sem.at[1])
    load_t.start()
    load_v.start()

    barrier = pltpu.get_barrier_semaphore()
    for shift in Z_SHIFTS:
        pl.semaphore_signal(barrier, 1, device_id=z_peer(shift), device_id_type=MESH)
    for shift in Y_SHIFTS:
        pl.semaphore_signal(barrier, 1, device_id=y_peer(shift), device_id_type=MESH)

    def greet(i, carry):
        pl.semaphore_signal(
            barrier, 1, device_id=(owner_at(i), blk), device_id_type=MESH
        )
        return carry

    lax.fori_loop(0, NCHAN - 1, greet, 0)

    places = [
        ((z - q // NY + NZ) % NZ) * NY + (y - q % NY + NY) % NY for q in range(NCHAN)
    ]

    def locate(d, carry):
        place = jnp.int32(0)
        for q in range(NCHAN):
            place = jnp.where(owner_ref[q] == d, places[q], place)
        slots[d] = place
        return carry

    lax.fori_loop(0, NCHAN, locate, 0)

    pl.semaphore_wait(barrier, len(Z_SHIFTS) + len(Y_SHIFTS) + NCHAN - 1)

    def piece(c):
        return pl.ds(c * PROWS, PROWS)

    def half(direction):
        return range(PIECES // 2) if direction == 0 else range(PIECES // 2, PIECES)

    def ring(buf, direction, hop, c, length, peer, s_sem, r_sem):
        sign = -1 if direction == 0 else 1
        src = t_ref.at[0] if hop == 1 else buf.at[(sign * (hop - 1)) % length]
        return pltpu.make_async_remote_copy(
            src_ref=src.at[piece(c)],
            dst_ref=buf.at[(sign * hop) % length, piece(c)],
            send_sem=s_sem.at[direction, hop - 1, c],
            recv_sem=r_sem.at[direction, hop - 1, c],
            device_id=peer(1 if direction == 0 else -1 + length),
            device_id_type=MESH,
        )

    z_last, y_last = NZ // 2, NY // 2
    z_copies = {
        (d, h, c): ring(tz, d, h, c, NZ, z_peer, zs_sem, zr_sem)
        for h in range(1, z_last + 1)
        for d in range(2)
        for c in (range(PIECES) if h < z_last else half(d))
    }
    y_copies = {
        (d, h, c): ring(ty, d, h, c, NY, y_peer, ys_sem, yr_sem)
        for h in range(1, y_last + 1)
        for d in range(2)
        for c in (range(PIECES) if h < y_last else half(d))
    }

    for c in range(PIECES):
        for d in range(2):
            z_copies[d, 1, c].start()
            y_copies[d, 1, c].start()

    def pass_on(copies, hop, c):
        for d in range(2):
            if (d, hop, c) in copies:
                copies[d, hop, c].wait_recv()
                if (d, hop + 1, c) in copies:
                    copies[d, hop + 1, c].start()

    load_v.wait()
    live = dims_ref[0]
    tile = 256
    for i in range(0, JAC, tile):
        row_ok = lax.broadcasted_iota(jnp.int32, (tile, tile), 0) + i < live
        for j in range(0, JAC, tile):
            col_ok = lax.broadcasted_iota(jnp.int32, (tile, tile), 1) + j < live
            a = v_raw[i : i + tile, j : j + tile].astype(jnp.float32)
            b = v_raw[j : j + tile, i : i + tile].astype(jnp.float32).T
            mean = jnp.where(row_ok & col_ok, (a + b) * 0.5, 0.0)
            v_sym[i : i + tile, j : j + tile] = mean.astype(jnp.bfloat16)

    def weigh(place, rows):
        for n in range(0, JAC, 256):
            wts[place * ROWS : (place + 1) * ROWS, n : n + 256] = jnp.dot(
                rows, v_sym[:, n : n + 256], preferred_element_type=jnp.float32
            ).astype(jnp.bfloat16)

    def product(first, count, cols):
        return lax.dot_general(
            wts[first * ROWS : (first + count) * ROWS, :],
            cols,
            (((1,), (1,)), ((), ())),
            preferred_element_type=jnp.float32,
        ).astype(jnp.bfloat16)

    def keep(block, dz, dy):
        for j in range(CHUNKS):
            got[j][dz, dy] = block[j * CROWS : (j + 1) * CROWS]

    def near(dz):
        keep(product(OWN, 1, tz[dz]), -dz % NZ, 0)

    def line(dy):
        made = product(0, OWN + 1, ty[dy])
        for s in range(OWN):
            for j in range(CHUNKS):
                at = s * ROWS + j * CROWS
                z_out[s, j, -dy % NY - 1] = made[at : at + CROWS]
        keep(made[OWN * ROWS :], 0, -dy % NY)

    def far(dz):
        made = product(OWN, 1 + len(Y_SHIFTS), tz[dz])
        keep(made[:ROWS], -dz % NZ, 0)
        for s in range(len(Y_SHIFTS)):
            for j in range(CHUNKS):
                at = (s + 1) * ROWS + j * CROWS
                y_out[s, j, FAR.index(-dz % NZ)] = made[at : at + CROWS]

    pass_on(z_copies, 1, 0)
    pass_on(z_copies, 1, 1)
    pass_on(y_copies, 1, 0)
    load_t.wait()
    weigh(OWN, tz[0])
    pass_on(z_copies, 1, 2)
    pass_on(z_copies, 1, 3)
    pass_on(y_copies, 1, 1)
    near(0)
    weigh(Z_SHIFTS.index(1), tz[1])
    pass_on(z_copies, 2, 0)
    weigh(Z_SHIFTS.index(7), tz[7])
    pass_on(z_copies, 2, 1)
    pass_on(y_copies, 1, 2)
    near(1)
    near(7)
    pass_on(z_copies, 2, 2)
    pass_on(z_copies, 2, 3)
    pass_on(y_copies, 1, 3)
    weigh(Z_SHIFTS.index(2), tz[2])
    pass_on(z_copies, 3, 0)
    weigh(Z_SHIFTS.index(6), tz[6])
    pass_on(z_copies, 3, 1)
    weigh(OWN + 1, ty[1])
    weigh(OWN + 3, ty[3])
    pass_on(z_copies, 3, 2)
    near(2)
    near(6)
    line(1)
    pass_on(z_copies, 3, 3)
    line(3)
    for c in range(PIECES):
        pass_on(y_copies, 2, c)
    line(2)

    z_sends = [
        [
            pltpu.make_async_remote_copy(
                src_ref=z_out.at[s, j],
                dst_ref=got[j].at[shift, pl.ds(1, NY - 1)],
                send_sem=xs_sem.at[j, s],
                recv_sem=xr_sem.at[j, s],
                device_id=z_peer(shift),
                device_id_type=MESH,
            )
            for s, shift in enumerate(Z_SHIFTS)
        ]
        for j in range(CHUNKS)
    ]
    y_sends = [
        [
            pltpu.make_async_remote_copy(
                src_ref=y_out.at[s, j],
                dst_ref=got[j].at[pl.ds(FAR[0], len(FAR)), shift],
                send_sem=xs_sem.at[j, OWN + s],
                recv_sem=xr_sem.at[j, OWN + s],
                device_id=y_peer(shift),
                device_id_type=MESH,
            )
            for s, shift in enumerate(Y_SHIFTS)
        ]
        for j in range(CHUNKS)
    ]
    for j in range(CHUNKS):
        for copy in z_sends[j]:
            copy.start()
    weigh(OWN + 2, ty[2])
    far(3)
    far(5)
    for c in range(PIECES):
        pass_on(z_copies, 4, c)
    far(4)
    for j in range(CHUNKS):
        for copy in y_sends[j]:
            copy.start()

    def to_owner(j, i):
        return pltpu.make_async_remote_copy(
            src_ref=stage[j].at[i],
            dst_ref=out_ref.at[0, chan, pl.ds(j * CROWS, CROWS)],
            send_sem=os_sem.at[j],
            recv_sem=or_sem.at[0],
            device_id=(owner_at(i), blk),
            device_id_type=MESH,
        )

    for j in range(CHUNKS):
        for copy in z_sends[j] + y_sends[j]:
            copy.wait_recv()

        def pick(i, carry):
            place = slots[owner_at(i)]
            stage[j][i] = got[j][place // NY, place % NY]
            return carry

        lax.fori_loop(0, NCHAN, pick, 0)

        def send(i, carry):
            to_owner(j, i).start()
            return carry

        lax.fori_loop(0, NCHAN - 1, send, 0)
        pltpu.make_async_copy(
            stage[j].at[NCHAN - 1],
            out_ref.at[0, chan, pl.ds(j * CROWS, CROWS)],
            or_sem.at[0],
        ).start()

    for copies in (z_copies, y_copies):
        for copy in copies.values():
            copy.wait_send()
    for j in range(CHUNKS):
        for copy in z_sends[j] + y_sends[j]:
            copy.wait_send()
        sent = stage[j].at[pl.ds(0, NCHAN - 1)]
        pltpu.make_async_copy(sent, sent, os_sem.at[j]).wait()
    pltpu.make_async_copy(out_ref, out_ref, or_sem.at[0]).wait()


def per_device(t_matrix, v_jacobi, channel_dims, owner_map):
    bf16 = jnp.bfloat16
    any_spec = pl.BlockSpec(memory_space=pl.ANY)
    smem_spec = pl.BlockSpec(memory_space=pltpu.SMEM)
    return pl.pallas_call(
        kernel,
        out_shape=jax.ShapeDtypeStruct((1, NCHAN, ROWS, CB), bf16),
        in_specs=[any_spec, any_spec, smem_spec, smem_spec],
        out_specs=any_spec,
        scratch_shapes=[
            pltpu.VMEM((NZ, ROWS, JAC), bf16),
            pltpu.VMEM((NY, ROWS, JAC), bf16),
            pltpu.VMEM((JAC, JAC), bf16),
            pltpu.VMEM((JAC, JAC), bf16),
            pltpu.VMEM(((OWN + 1 + len(Y_SHIFTS)) * ROWS, JAC), bf16),
            pltpu.VMEM((OWN, CHUNKS, NY - 1, CROWS, CB), bf16),
            pltpu.VMEM((len(Y_SHIFTS), CHUNKS, len(FAR), CROWS, CB), bf16),
        ]
        + [pltpu.VMEM((NZ, NY, CROWS, CB), bf16)] * CHUNKS
        + [pltpu.VMEM((NCHAN, CROWS, CB), bf16)] * CHUNKS
        + [
            pltpu.SMEM((NCHAN,), jnp.int32),
            pltpu.SemaphoreType.DMA((2,)),
            pltpu.SemaphoreType.DMA((2, NZ // 2, PIECES)),
            pltpu.SemaphoreType.DMA((2, NZ // 2, PIECES)),
            pltpu.SemaphoreType.DMA((2, NY // 2, PIECES)),
            pltpu.SemaphoreType.DMA((2, NY // 2, PIECES)),
            pltpu.SemaphoreType.DMA((CHUNKS, OWN + len(Y_SHIFTS))),
            pltpu.SemaphoreType.DMA((CHUNKS, OWN + len(Y_SHIFTS))),
            pltpu.SemaphoreType.DMA((CHUNKS,)),
            pltpu.SemaphoreType.DMA((1,)),
        ],
        compiler_params=pltpu.CompilerParams(collective_id=0, has_side_effects=True),
        name="lab_blocks",
    )(t_matrix, v_jacobi, channel_dims, owner_map)


def solution(mesh):
    in_specs = (P("chan", "blk", None), P("chan", None, None), P("chan"), P())
    out_specs = P("chan", None, "blk", None)
    return jax.shard_map(
        per_device, mesh=mesh, in_specs=in_specs, out_specs=out_specs, check_vma=False
    )
```

time: 225 us -> 83.2 us (0.37)
  waiting for transfers between devices: 155 us -> 0 us
  Pallas kernels: 0 us -> 79.7 us
  blocking collectives: 39.6 us -> 0 us
  between operations: 14.1 us -> 0.66 us
  matrix products: 9.23 us -> 0 us
  local copies, waits for them, and re-layouts: 6.14 us -> 2.31 us
    all_gather x1 -> x0, waiting for transfers between devices: 155 us -> none  [per_device(): lax.all_gather(t_matrix, 'blk', axis=1, tiled=True)]
    pallas_call x0 -> x1, Pallas kernels: none -> 79.7 us  [per_device(): pl.pallas_call(kernel, out_shape=jax.ShapeDtypeStruct((1, NCHAN, ROWS, CB...]
    all_to_all x1 -> x0, blocking collectives: 39.6 us -> none  [per_device(): lax.all_to_all(outgoing, 'chan', split_axis=0, concat_axis=1, tiled=True)]
    dot_general x1 -> x0, matrix products: 9.23 us -> none  [per_device(): jnp.einsum('cri,cpi->crp', weighted, lax.all_gather(t_matrix, 'blk', axis...]
    convert_element_type x1 -> x0, local copies, waits for them, and re-layouts: 4.13 us -> none  [per_device(): v_float = v_jacobi.astype(jnp.float32)]
  transfers between devices with their start and end apart: 1 -> 0, of which waited for: 1 -> 0; matrix products, arithmetic and copies ran while one was open for 2% -> 0% of each run, Pallas kernels for 0% -> 0%
where the time goes in v1:
time: 83.2 us; the launch traced here: 82.7 us
  Pallas kernels  79.7 us (96%)
  local copies, waits for them, and re-layouts  2.31 us (3%)
    pallas_call x1, Pallas kernels, per_device(): pl.pallas_call(kernel, out_shape=jax.ShapeDtypeStruct((1, NCHAN, ROWS, CB...  79.7 us
    unnamed x1, local copies, waits for them, and re-layouts  2.31 us

profile of v1, /device:TPU:1, one launch (start us, length us, event | category | flops | bytes accessed | tf_op | source)
XLA Modules:
  0.0 82.7 jit_solution(7238969935881114512)
XLA Ops:
  0.7 79.7 %lab_blocks.1 = bf16[1,32,128,128]{3,2,1,0:T(8,128)(2,1)} custom-call(bf16[1,128,1024]{2,1,0:T(8,128)(2,1)} %t_ref.1, bf16[1,1024,1024]{2,1,0:T(8,128)(2,1)} %v_ref.1, s32[1]{0:T(128)S(6)} %copy.6.dims_ref, s32[32]{0:T(128)} %owner_ref.1), custom_call_target="tpu_custom_call" | custom-call | tf_op jit(solution)/shard_map/lab_blocks/pallas_call | solution.py:319
  80.3 2.3 %copy.7 = bf16[1,32,128,128]{3,2,1,0:T(8,128)(2,1)} copy(bf16[1,32,128,128]{3,2,1,0:T(8,128)(2,1)} %lab_blocks.1) | data formatting | bytes 2097152

commit v2 on v1

--- a/solution.py
+++ b/solution.py
@@ -62,7 +62,7 @@
         return (chan, z * NY + (y + shift) % NY)
 
     def owner_at(i):
-        k, b = i % NX, 3 - i // NX
+        k, b = i // (NL * NC), NL * NC - 1 - i % (NL * NC)
         dx = NX // 2 + (1 - 2 * (k % 2)) * ((k + 1) // 2)
         return (((x + dx) % NX) * NL + (lo + b // 2) % NL) * NC + (core + b % 2) % NC
 
@@ -344,7 +344,9 @@
             pltpu.SemaphoreType.DMA((CHUNKS,)),
             pltpu.SemaphoreType.DMA((1,)),
         ],
-        compiler_params=pltpu.CompilerParams(collective_id=0, has_side_effects=True),
+        compiler_params=pltpu.CompilerParams(
+            collective_id=0, has_side_effects=True, vmem_limit_bytes=52 * 2**20
+        ),
         name="lab_blocks",
     )(t_matrix, v_jacobi, channel_dims, owner_map)
 

time: 83.2 us -> 82.5 us (level)
    unnamed x1 -> x5, local copies, waits for them, and re-layouts: 2.31 us -> 2.57 us
where the time goes in v2:
time: 82.5 us; the launch traced here: 82.3 us
  Pallas kernels  79.1 us (96%)
  local copies, waits for them, and re-layouts  2.57 us (3%)
    pallas_call x1, Pallas kernels, per_device(): pl.pallas_call(kernel, out_shape=jax.ShapeDtypeStruct((1, NCHAN, ROWS, CB...  79.1 us
    unnamed x5, local copies, waits for them, and re-layouts  2.57 us

profile of v2, /device:TPU:1, one launch (start us, length us, event | category | flops | bytes accessed | tf_op | source)
XLA Modules:
  0.0 82.3 jit_solution(18355600084358179444)
XLA Ops:
  0.7 0.0 copy-start
  0.7 0.9 %copy-done = bf16[1,128,1024]{2,1,0:T(8,128)(2,1)S(1)} copy-done((bf16[1,128,1024]{2,1,0:T(8,128)(2,1)S(1)}, bf16[1,128,1024]{2,1,0:T(8,128)(2,1)}, u32[]{:S(2)}) %copy-start) | copy-done | bytes 262168
  1.6 0.0 copy-start.1
  1.6 0.7 copy-done.1
  2.3 79.1 %lab_blocks.1 = bf16[1,32,128,128]{3,2,1,0:T(8,128)(2,1)S(1)} custom-call(bf16[1,128,1024]{2,1,0:T(8,128)(2,1)S(1)} %copy-done, bf16[1,1024,1024]{2,1,0:T(8,128)(2,1)} %v_ref.1, s32[1]{0:T(128)S(6)} %copy.6.dims_ref, s32[32]{0:T(128)S(1)} %copy-done.1), custom_call_target="tpu_custom_call" | custom-call | tf_op jit(solution)/shard_map/lab_blocks/pallas_call | solution.py:319
  81.3 1.0 %copy.7 = bf16[1,32,128,128]{3,2,1,0:T(8,128)(2,1)} copy(bf16[1,32,128,128]{3,2,1,0:T(8,128)(2,1)S(1)} %lab_blocks.1) | data formatting | bytes 2097152
Async XLA Ops:
  0.7 1.0 %copy-start = (bf16[1,128,1024]{2,1,0:T(8,128)(2,1)S(1)}, bf16[1,128,1024]{2,1,0:T(8,128)(2,1)}, u32[]{:S(2)}) copy-start(bf16[1,128,1024]{2,1,0:T(8,128)(2,1)} %t_ref.1) | copy-start | bytes 786436
  1.6 0.7 copy-start.1
